TPU v7x, 32 devices: a whole 2x2x4 slice. The times are simulated.
32 devices in a mesh: section: 2 (over core), fsdp: 4 (over z), dp: 4 (over y, x).
Axes of the slice: x: 2, y: 2, z: 4, core: 2. Of those that a mesh axis runs over, the one named last changes fastest.
Arguments:
- tokens: bfloat16 [1, 16, 128, 1024], P(None, ('fsdp', 'dp')), may hold values from -6 to 6
- segments: int32 [1, 16, 128], P(None, ('fsdp', 'dp')), may hold values from 0 to 3, never falling along the last dimension, each value on 1 to 64 neighbouring positions
- cotangent: float32 [1, 16, 128, 1024], P(None, ('fsdp', 'dp')), may hold values from -6 to 6
- norm_gains: bfloat16 [2, 2, 1024], P('section', None, 'fsdp'), may hold values from 0.5 to 1.5
- proj_weight: bfloat16 [2, 1024, 3072], P('section', 'fsdp'), may hold values from -0.1875 to 0.1875
- rate_weight: bfloat16 [2, 1024, 8], P('section', 'fsdp'), may hold values from -0.1875 to 0.1875
- out_weight: bfloat16 [2, 1024, 1024], P('section', 'fsdp'), may hold values from -0.375 to 0.375
- up_weight: bfloat16 [2, 1024, 5632], P('section', 'fsdp'), may hold values from -0.1875 to 0.1875
- down_weight: bfloat16 [2, 1024, 2816], P('section', 'fsdp'), may hold values from -0.21875 to 0.21875
- conv_kernels: float32 [2, 4, 2048], P('section'), may hold values from -3 to 3
- head_params: float32 [2, 2, 4], P('section'), may hold values from -2.5 to 0.5
- out_gain: float32 [2, 256], P('section'), may hold values from 0.5 to 1.5
Outputs:
- section_output: bfloat16 [2, 1, 16, 128, 1024], P('section', None, ('fsdp', 'dp'))
- input_grad: float32 [2, 1, 16, 128, 1024], P('section', None, ('fsdp', 'dp'))
- gains_grad: float32 [2, 2, 1024], P('section', None, 'fsdp')
- proj_grad: float32 [2, 1024, 3072], P('section', 'fsdp')
- rate_grad: float32 [2, 1024, 8], P('section', 'fsdp')
- out_grad: float32 [2, 1024, 1024], P('section', 'fsdp')
- up_grad: float32 [2, 1024, 5632], P('section', 'fsdp')
- down_grad: float32 [2, 1024, 2816], P('section', 'fsdp')
- kernel_grad: float32 [2, 4, 2048], P('section')
- head_grad: float32 [2, 2, 4], P('section')
- out_gain_grad: float32 [2, 256], P('section')
Inputs may be any that keep to these rules, and one draw needn't show every extreme that they name: `segments`: within each sequence the numbers never fall, every one of 0 .. 3 occurs, and each document holds 1 to 64 positions, one exactly 64.
All inputs are finite; a program needn't handle non-finite values.
Results may differ from a plain program's by a relative error of at most 0.034.
Values may be sent and summed in bfloat16 or wider, within the bound.
A program may use at most 256 MiB of HBM per device.

v0:
```python
from functools import partial

import jax
import jax.numpy as jnp
from jax import lax
from jax.sharding import PartitionSpec as P

SPAN = 64


highest = lax.Precision.HIGHEST
reset_level = -30.0


def passed_along(value, axis, steps):
    count = lax.axis_size(axis)
    leading, last = (max(0, -steps), min(count, count - steps))
    return lax.ppermute(value, axis, [(source, source + steps) for source in range(leading, last)])


def rms_gain(values, gain_vec):
    return values * lax.rsqrt(jnp.mean(values * values, -1, keepdims=True) + 1e-06) * gain_vec


def swiglu(joined):
    half_width = joined.shape[-1] // 2
    return jax.nn.silu(joined[..., :half_width]) * joined[..., half_width:]


def short_conv(raw_input, kernel, segment):
    length = raw_input.shape[1]
    tap_count = kernel.shape[0]
    total = raw_input * kernel[tap_count - 1]
    for offset in range(1, tap_count):
        shifted = jnp.pad(raw_input, ((0, 0), (offset, 0), (0, 0)))[:, :length]
        earlier = jnp.pad(segment, ((0, 0), (offset, 0)), constant_values=-1)[:, :length]
        total = (
            total
            + jnp.where((earlier == segment)[..., None], shifted, 0.0)
            * kernel[tap_count - 1 - offset]
        )
    return jax.nn.silu(total)


def delta_rule(queries, key_rows, value_rows, beta_gate, decays, block_len):
    batch_size, head_count, length, key_dim = queries.shape
    value_dim = value_rows.shape[-1]
    block_count = length // block_len

    def to_blocks(array):
        return array.reshape(array.shape[:2] + (block_count, block_len) + array.shape[3:])

    queries = to_blocks(queries)
    key_rows = to_blocks(key_rows)
    value_rows = to_blocks(value_rows)
    beta_gate = to_blocks(beta_gate)
    levels = jnp.cumsum(to_blocks(decays), axis=-1)
    places = jnp.arange(block_len)
    lower_mask = places[:, None] >= places[None, :]
    strict_mask = places[:, None] > places[None, :]
    spread = jnp.exp(jnp.where(lower_mask, levels[..., :, None] - levels[..., None, :], -1e30))
    beta_keys = key_rows * beta_gate[..., None]
    key_inner = jnp.einsum("bhncd,bhnmd->bhncm", beta_keys, key_rows, precision=highest) * spread
    system = jnp.where(strict_mask, key_inner, 0.0)
    right_side = jnp.concatenate(
        [beta_keys * jnp.exp(levels)[..., None], value_rows * beta_gate[..., None]], -1
    )
    solved = lax.linalg.triangular_solve(
        system, right_side, left_side=True, lower=True, unit_diagonal=True
    )
    solved_keys = solved[..., :key_dim]
    solved_values = solved[..., key_dim:]
    scores = jnp.einsum("bhncd,bhnmd->bhncm", queries, key_rows, precision=highest) * spread
    fading = queries * jnp.exp(levels)[..., None]
    final_level = levels[..., -1:]
    carried = key_rows * jnp.exp(final_level - levels)[..., None]

    def advance(memory, pieces):
        fading_part, keys_part, values_part, scores_part, carried_part, final_part = pieces
        update = values_part - jnp.einsum("bhcd,bhde->bhce", keys_part, memory, precision=highest)
        output = jnp.einsum("bhcd,bhde->bhce", fading_part, memory, precision=highest) + jnp.einsum(
            "bhcm,bhme->bhce", scores_part, update, precision=highest
        )
        memory = memory * jnp.exp(final_part)[..., None] + jnp.einsum(
            "bhcd,bhce->bhde", carried_part, update, precision=highest
        )
        return (memory, output)

    pieces = tuple(
        (
            jnp.moveaxis(array, 2, 0)
            for array in (fading, solved_keys, solved_values, scores, carried, final_level)
        )
    )
    initial = jnp.zeros((batch_size, head_count, key_dim, value_dim), queries.dtype)
    _, outputs = lax.scan(advance, initial, pieces)
    return jnp.moveaxis(outputs, 0, 2).reshape(batch_size, head_count, length, value_dim)


def token_mixer(projected, rate_logits, kernel, head_params, out_gain, segment):
    batch_size, length, _ = projected.shape
    head_count = head_params.shape[1]
    value_dim = out_gain.shape[0]
    channels = kernel.shape[1]
    key_width = (channels - head_count * value_dim) // 2
    key_dim = key_width // head_count
    mixed = short_conv(projected[..., :channels], kernel, segment)

    def heads_of(array, size):
        return jnp.moveaxis(array.reshape(batch_size, length, head_count, size), 2, 1)

    queries = heads_of(mixed[..., :key_width], key_dim)
    key_rows = heads_of(mixed[..., key_width : 2 * key_width], key_dim)
    value_rows = heads_of(mixed[..., 2 * key_width :], value_dim)
    queries = (
        queries
        * lax.rsqrt(jnp.sum(queries * queries, -1, keepdims=True) + 1e-06)
        * key_dim ** (-0.5)
    )
    key_rows = key_rows * lax.rsqrt(jnp.sum(key_rows * key_rows, -1, keepdims=True) + 1e-06)
    beta_gate = jax.nn.sigmoid(jnp.moveaxis(rate_logits[..., head_count:], 2, 1))
    decays = -jnp.exp(head_params[0])[:, None] * jax.nn.softplus(
        jnp.moveaxis(rate_logits[..., :head_count], 2, 1) + head_params[1][:, None]
    )
    earlier = jnp.pad(segment, ((0, 0), (1, 0)), constant_values=-1)[:, :length]
    decays = jnp.where((earlier != segment)[:, None, :], reset_level, decays)
    output = delta_rule(queries, key_rows, value_rows, beta_gate, decays, SPAN)
    output = output * lax.rsqrt(jnp.mean(output * output, -1, keepdims=True) + 1e-05) * out_gain
    gating = heads_of(projected[..., channels:], value_dim)
    return jnp.moveaxis(output * jax.nn.silu(gating), 1, 2).reshape(
        batch_size, length, head_count * value_dim
    )


def last_contract(left, right):
    return lax.dot_general(
        left, right, (((2,), (1,)), ((), ())), preferred_element_type=jnp.float32
    )


def layer_forward(entering, segment, weights, small_params):
    norm_gains, proj_weight, rate_weight, out_weight, up_weight, down_weight = weights
    kernel, head_params, out_gain = small_params
    widened = entering.astype(jnp.float32)
    normed_one, norm_one_back = jax.vjp(rms_gain, widened, norm_gains[0].astype(jnp.float32))
    hidden_one = normed_one.astype(jnp.bfloat16)
    projected = jnp.dot(hidden_one, proj_weight, preferred_element_type=jnp.float32)
    rate_logits = jnp.dot(hidden_one, rate_weight, preferred_element_type=jnp.float32)
    mixed_out, mixer_back = jax.vjp(
        partial(token_mixer, segment=segment), projected, rate_logits, kernel, head_params, out_gain
    )
    mixed_half = mixed_out.astype(jnp.bfloat16)
    stream = widened + last_contract(mixed_half, out_weight)
    normed_two, norm_two_back = jax.vjp(rms_gain, stream, norm_gains[1].astype(jnp.float32))
    hidden_two = normed_two.astype(jnp.bfloat16)
    gate_up = jnp.dot(hidden_two, up_weight, preferred_element_type=jnp.float32)
    activated, act_back = jax.vjp(swiglu, gate_up)
    act_half = activated.astype(jnp.bfloat16)
    layer_out = (stream + last_contract(act_half, down_weight)).astype(jnp.bfloat16)
    residuals = (
        norm_one_back,
        hidden_one,
        mixer_back,
        mixed_half,
        norm_two_back,
        hidden_two,
        act_back,
        act_half,
    )
    return (layer_out, residuals)


def layer_backward(cotangent_in, residuals, weights):
    norm_gains, proj_weight, rate_weight, out_weight, up_weight, down_weight = weights
    (
        norm_one_back,
        hidden_one,
        mixer_back,
        mixed_half,
        norm_two_back,
        hidden_two,
        act_back,
        act_half,
    ) = residuals
    dout_half = cotangent_in.astype(jnp.bfloat16)
    (gate_up_grad,) = act_back(jnp.dot(dout_half, down_weight, preferred_element_type=jnp.float32))
    gate_up_cot = gate_up_grad.astype(jnp.bfloat16)
    stream_grad, gain_two = norm_two_back(last_contract(gate_up_cot, up_weight))
    stream_grad = cotangent_in + stream_grad
    branch_cot = stream_grad.astype(jnp.bfloat16)
    proj_grad, rate_grad, kernel_grad, head_grad, out_gain_grad = mixer_back(
        jnp.dot(branch_cot, out_weight, preferred_element_type=jnp.float32)
    )
    proj_cot = proj_grad.astype(jnp.bfloat16)
    rate_cot = rate_grad.astype(jnp.bfloat16)
    hidden_grad = last_contract(proj_cot, proj_weight) + last_contract(rate_cot, rate_weight)
    entry_grad, gain_one = norm_one_back(hidden_grad)
    pairs = (
        hidden_one,
        proj_cot,
        rate_cot,
        mixed_half,
        branch_cot,
        hidden_two,
        gate_up_cot,
        act_half,
        dout_half,
    )
    return (
        stream_grad + entry_grad,
        pairs,
        (kernel_grad, head_grad, out_gain_grad),
        jnp.stack([gain_one, gain_two]),
    )


def weight_terms(pairs, gain_sum, start, count):
    flattened = [member.reshape(-1, member.shape[-1]) for member in pairs]
    (
        hidden_one,
        proj_cot,
        rate_cot,
        mixed_half,
        branch_cot,
        hidden_two,
        gate_up_cot,
        act_half,
        dout_half,
    ) = flattened

    def product(left, right):
        return lax.dot_general(
            left, right, (((0,), (0,)), ((), ())), preferred_element_type=jnp.float32
        )

    return jnp.concatenate(
        [
            product(hidden_one, proj_cot),
            product(hidden_one, rate_cot),
            product(branch_cot, mixed_half),
            product(hidden_two, gate_up_cot),
            product(dout_half, act_half),
            gain_sum.T,
        ],
        1,
    )


def split_term(total, widths):
    pieces = []
    column = 0
    for width in widths:
        pieces.append(total[..., column : column + width])
        column = column + width
    return pieces


def pass_forward(layer_out):
    return passed_along(layer_out, "section", 1)


def pass_backward(entry_grad):
    return passed_along(entry_grad.astype(jnp.bfloat16), "section", -1).astype(entry_grad.dtype)


def shards(
    tokens,
    segments,
    cotangent,
    norm_gains,
    proj_weight,
    rate_weight,
    out_weight,
    up_weight,
    down_weight,
    conv_kernels,
    head_params,
    out_gain,
):
    first_section = lax.axis_index("section") == 0
    weights = (
        lax.all_gather(norm_gains[0], "fsdp", axis=1, tiled=True),
        lax.all_gather(proj_weight[0], "fsdp", axis=0, tiled=True),
        lax.all_gather(rate_weight[0], "fsdp", axis=0, tiled=True),
        lax.all_gather(out_weight[0], "fsdp", axis=0, tiled=True),
        lax.all_gather(up_weight[0], "fsdp", axis=0, tiled=True),
        lax.all_gather(down_weight[0], "fsdp", axis=0, tiled=True),
    )
    small_params = (conv_kernels[0], head_params[0], out_gain[0])
    batches = tokens.shape[0]
    records = []
    results = []
    for forward_step in range(batches + 1):
        ahead_batch = min(forward_step, batches - 1)
        behind = max(forward_step - 1, 0)
        segment = jnp.where(first_section, segments[ahead_batch], segments[behind])
        if forward_step == 0:
            entering = tokens[0]
        else:
            entering = jnp.where(first_section, tokens[ahead_batch], pass_forward(results[-1]))
        produced, residuals = layer_forward(entering, segment, weights, small_params)
        records.append(residuals)
        results.append(produced)
    incoming = []
    kept_pairs = []
    small_list = []
    gain_list = []
    for backward_step in range(batches + 1):
        if backward_step < batches:
            own_cot = cotangent[batches - 1 - backward_step]
        else:
            own_cot = jnp.zeros_like(cotangent[0])
        if backward_step == 0:
            upstream = jnp.zeros_like(own_cot)
        else:
            upstream = pass_backward(incoming[-1])
        dout_full = jnp.where(first_section, upstream, own_cot)
        entry_grad, pairs, small_grads, gains_step = layer_backward(
            dout_full, records[batches - backward_step], weights
        )
        incoming.append(entry_grad)
        kept_pairs.append(pairs)
        small_list.append(small_grads)
        gain_list.append(gains_step)
    pairs_all = tuple((jnp.concatenate([member[i] for member in kept_pairs], 1) for i in range(9)))
    gain_sum = sum(gain_list)
    small_sum = tuple((sum((member[i] for member in small_list)) for i in range(3)))
    section_output = jnp.stack([jnp.where(first_section, results[0], results[1])])[None]
    input_grad = jnp.stack([jnp.where(first_section, incoming[batches], incoming[batches - 1])])[
        None
    ]
    own_rows = proj_weight.shape[1]
    term_of = partial(weight_terms, pairs_all, gain_sum)
    totals = lax.psum_scatter(
        term_of(jnp.int32(0), own_rows * lax.axis_size("fsdp")).astype(jnp.bfloat16),
        "fsdp",
        scatter_dimension=0,
        tiled=True,
    ).astype(jnp.float32)
    totals = lax.psum(totals.astype(jnp.bfloat16), "dp").astype(jnp.float32)
    kernel_grad, head_grad, out_gain_grad = lax.psum(
        (small_sum[0], small_sum[1], small_sum[2]), ("fsdp", "dp")
    )
    widths = [
        proj_weight.shape[2],
        rate_weight.shape[2],
        out_weight.shape[2],
        up_weight.shape[2],
        down_weight.shape[2],
        2,
    ]
    pieces = split_term(totals, widths)
    return (
        section_output,
        input_grad,
        pieces[5].T[None],
        pieces[0][None],
        pieces[1][None],
        pieces[2][None],
        pieces[3][None],
        pieces[4][None],
        kernel_grad[None],
        head_grad[None],
        out_gain_grad[None],
    )


def solution(mesh):
    return jax.shard_map(
        shards,
        mesh=mesh,
        in_specs=(
            P(None, ("fsdp", "dp"), None, None),
            P(None, ("fsdp", "dp"), None),
            P(None, ("fsdp", "dp"), None, None),
            P("section", None, "fsdp"),
            P("section", "fsdp", None),
            P("section", "fsdp", None),
            P("section", "fsdp", None),
            P("section", "fsdp", None),
            P("section", "fsdp", None),
            P("section", None, None),
            P("section", None, None),
            P("section", None),
        ),
        out_specs=(
            P("section", None, ("fsdp", "dp"), None, None),
            P("section", None, ("fsdp", "dp"), None, None),
            P("section", None, "fsdp"),
            P("section", "fsdp", None),
            P("section", "fsdp", None),
            P("section", "fsdp", None),
            P("section", "fsdp", None),
            P("section", "fsdp", None),
            P("section", None, None),
            P("section", None, None),
            P("section", None),
        ),
        check_vma=False,
    )
```

profile of v0, /device:TPU:0, one launch (start us, length us, event | category | flops | bytes accessed | tf_op | source)
XLA Modules:
  0.0 1455.4 jit_solution(11192671535240137623)
XLA Ops:
  10.3 12.7 all-gather
  23.2 13.7 all-gather.1
  41.3 86.5 %all-gather.11.cloned.1.call-done = bf16[1,1024,3072]{2,1,0:T(8,128)(2,1)} async-done(((bf16[1,256,3072]{2,1,0:T(8,128)(2,1)}), bf16[1,1024,3072]{2,1,0:T(8,128)(2,1)}) %all-gather.11.cloned.1.call-update) | async-done | bytes 6291472 | tf_op jit(solution)/shard_map/all_gather | solution.py:283
  127.9 3.8 fusion.194
  141.4 39.3 %custom-call.16 = f32[1,4,2,1,64,64]{4,5,3,2,1,0:T(8,128)S(1)} custom-call(f32[1,4,2,1,64,64]{5,4,3,2,1,0:T(8,128)S(1)} %fusion.409), custom_call_target="InvertDiagBlocksLowerTriangular" | custom-call | tf_op jit(solution)/shard_map/jvp()/triangular_solve/custom-call.1 | solution.py:68
  185.2 7.1 while.96
  195.3 2.0 multiply_convert_fusion.5
  199.1 2.6 multiply_reduce_fusion.16
  201.8 173.0 %all-gather.15.cloned.1.call-done = bf16[1,1024,5632]{2,1,0:T(8,128)(2,1)} async-done(((bf16[1,256,5632]{2,1,0:T(8,128)(2,1)}), bf16[1,1024,5632]{2,1,0:T(8,128)(2,1)}) %all-gather.15.cloned.1.call-update) | async-done | bytes 11534352 | tf_op jit(solution)/shard_map/all_gather | solution.py:286
  374.8 6.0 fusion.166
  382.8 98.3 %all-gather.17.cloned.1.call-done = bf16[1,1024,2816]{2,1,0:T(8,128)(2,1)} async-done(((bf16[1,256,2816]{2,1,0:T(8,128)(2,1)}), bf16[1,1024,2816]{2,1,0:T(8,128)(2,1)}) %all-gather.17.cloned.1.call-update) | async-done | bytes 5767184 | tf_op jit(solution)/shard_map/all_gather | solution.py:287
  481.2 4.6 fusion.242
  487.7 3.9 copy.525
  493.1 3.8 fusion.197
  498.8 2.0 fusion.283
  508.6 2.2 reshape.2341
  510.8 2.0 broadcast_multiply_fusion
  515.8 40.7 %custom-call.17 = f32[1,4,2,1,64,64]{4,5,3,2,1,0:T(8,128)} custom-call(f32[1,4,2,1,64,64]{5,4,3,2,1,0:T(8,128)} %fusion.397), custom_call_target="InvertDiagBlocksLowerTriangular" | custom-call | tf_op jit(solution)/shard_map/jvp()/triangular_solve/custom-call.1 | solution.py:68
  558.2 2.0 fusion.288
  576.0 11.5 while.97
  577.6 2.1 bitcast_dynamic-update-slice_fusion.14
  583.2 2.1 bitcast_dynamic-update-slice_fusion.14
  593.1 2.0 multiply_convert_fusion.3
  596.9 2.7 multiply_reduce_fusion.14
  599.8 6.1 fusion.169
  606.0 2.3 fusion.437
  608.5 4.4 fusion.349
  622.0 26.4 %while.98 = (s32[]{:T(128)}, f32[1,4,128,256]{2,3,1,0:T(8,128)S(1)}, f32[2,1,4,64,128]{4,3,0,2,1:T(8,128)}, f32[2,1,4,64,128]{4,3,2,1,0:T(8,128)}, f32[2,1,4,64,...) while((s32[]{:T(128)}, ...), condition=%wide.region_20.23_spmd.clone, body=%wide.region_18.22_spmd.clone.sunk | while | flops 706019328 | bytes 25702096 | solution.py:96
  622.8 2.1 copy.840
  626.2 2.1 fusion.662
  636.0 2.1 copy.840
  639.3 2.1 fusion.662
  648.4 3.2 fusion.296
  651.7 2.8 convolution_bitcast_fusion.17
  663.8 2.0 fusion.363
  667.7 2.4 fusion.539
  678.4 2.6 multiply_select_fusion.3
  690.0 2.7 fusion.275
  693.7 2.2 fusion.174
  702.5 4.9 fusion.436
  708.3 3.7 fusion.158
  720.9 19.1 %while.99 = (s32[]{:T(128)}, f32[1,4,128,256]{2,3,1,0:T(8,128)S(1)}, f32[2,1,4,64,128]{4,3,0,2,1:T(8,128)}, f32[2,1,4,64,128]{4,3,2,1,0:T(8,128)}, f32[2,1,4,64,...) while((s32[]{:T(128)}, ...), condition=%wide.region_37.42_spmd.clone, body=%wide.region_35.41_spmd.clone.sunk | while | flops 706019328 | bytes 25701472 | solution.py:96
  721.3 2.1 fusion.683
  730.6 2.2 fusion.683
  740.0 2.5 fusion.293
  751.6 2.2 fusion.376
  762.4 5.6 multiply_reduce_fusion.3
  774.6 1.9 reduce_window_sum.43
  777.6 2.4 fusion.278
  781.0 2.2 fusion.172
  785.2 4.5 convolution_convert_fusion.2
  790.0 2.0 convolution_convert_fusion.3
  792.1 4.1 copy.594
  796.2 7.3 convolution_convert_fusion
  803.8 5.7 convolution_convert_fusion.1
  809.5 48.0 %concatenate.48 = bf16[1024,12554]{1,0:T(8,128)(2,1)} concatenate(bf16[1024,3072]{1,0:T(8,128)(2,1)} %convolution_convert_fusion.2, bf16[1024,8]{1,0:T(8,128)(2,1)S(1)} %copy.593, bf16[1024,1024]{1,0:T(8,128)(2,1)S(1)} %copy-done.42, bf16[1024,5632]{1,0:T(8,128)(2,1)} %convolution_convert_fusion, bf16[1024,2816]{1,0:T(8,128)(2,1)} %convolution_convert_fusion.1, ...), dimensions={1} | concatenate | bytes 51421184 | tf_op jit(solution)/shard_map/concatenate | solution.py:236
  857.5 427.1 %reduce-scatter.2.cloned.1.call-done = bf16[256,12554]{1,0:T(8,128)(2,1)} async-done(((bf16[1024,12554]{1,0:T(8,128)(2,1)}), bf16[256,12554]{1,0:T(8,128)(2,1)}) %reduce-scatter.2.cloned.1.call-update) | async-done | bytes 6427664 | tf_op jit(solution)/shard_map/reduce_scatter | solution.py:334
  1285.9 5.3 fusion.264
  1291.4 79.9 %all-reduce.51 = (f32[1,4,2048]{2,1,0:T(4,128)}, f32[1,2,4]{2,1,0:T(2,128)}, f32[1,256]{1,0:T(1,128)}) all-reduce(f32[1,4,2048]{2,1,0:T(4,128)S(1)} %add_bitcast_fusion.2, f32[1,2,4]{2,1,0:T(2,128)S(1)} %add_bitcast_fusion.3, f32[1,256]{1,0:T(1,128)S(1)} %bitcast.1621), channel_id=1, replica_groups=mesh['section'=2,'fsdp'=4,'dp'=4] {'fsdp','dp'}, use_global_device_ids=true, to_apply=%region_64.69 | all-reduce | flops 8456 | bytes 67648 | tf_op jit(solution)/shard_map/psum | solution.py:341
  1371.3 62.1 %all-reduce.54.cloned.1.call-done = bf16[256,12554]{1,0:T(8,128)(2,1)} async-done(((bf16[256,12554]{1,0:T(8,128)(2,1)}), bf16[256,12554]{1,0:T(8,128)(2,1)}) %all-reduce.54.cloned.1.call-update) | async-done | bytes 6427664 | tf_op jit(solution)/shard_map/psum | solution.py:340
  1433.4 3.7 convert_element_type.239
  1437.2 2.0 slice_bitcast_fusion.1
  1440.6 4.1 slice_bitcast_fusion
  1444.6 2.4 slice_bitcast_fusion.2
  (1014 shorter events, 200.4 us)
Async XLA Ops:
  7.2 120.7 %all-gather.11.cloned.1.call-start = ((), (), s32[]{:S(2)}) async-start(), calls=%async_computation.3 | async-start | bytes 7864320 | tf_op jit(solution)/shard_map/all_gather | solution.py:283
  7.9 191.2 %all-gather.13.cloned.1.call-start = ((), (), s32[]{:S(2)}) async-start(), calls=%async_computation.4 | async-start | bytes 2621440 | tf_op jit(solution)/shard_map/all_gather | solution.py:285
  8.7 14.3 copy-start.17
  8.7 14.5 copy-start.258
  8.7 31.9 %copy-start.193 = (f32[1,4,2048]{2,1,0:T(4,128)S(1)}, f32[1,4,2048]{2,1,0:T(4,128)}, u32[]{:S(2)}) copy-start(f32[1,4,2048]{2,1,0:T(4,128)} %param.36) | copy-start | bytes 98308
  8.7 366.1 %all-gather.15.cloned.1.call-start = ((), (), s32[]{:S(2)}) async-start(), calls=%async_computation.5 | async-start | bytes 14417920 | tf_op jit(solution)/shard_map/all_gather | solution.py:286
  9.5 471.7 %all-gather.17.cloned.1.call-start = ((), (), s32[]{:S(2)}) async-start(), calls=%async_computation.6 | async-start | bytes 7208960 | tf_op jit(solution)/shard_map/all_gather | solution.py:287
  10.0 1274.5 %reduce-scatter.2.cloned.1.call-start = ((), (), s32[]{:S(2)}) async-start(), calls=%async_computation.1 | async-start | bytes 32440320 | tf_op jit(solution)/shard_map/reduce_scatter | solution.py:334
  10.1 130.4 %copy-start.154 = (f32[64,64]{1,0:T(8,128)}, f32[64,64]{1,0:T(8,128)S(1)}, u32[]{:S(2)}) copy-start(f32[64,64]{1,0:T(8,128)S(1)} %get-tuple-element.1668) | copy-start | bytes 49156
  10.1 130.4 %copy-start.161 = (pred[64,64]{1,0:T(8,128)(4,1)}, pred[64,64]{1,0:T(8,128)(4,1)S(1)}, u32[]{:S(2)}) copy-start(pred[64,64]{1,0:T(8,128)(4,1)S(1)} %get-tuple-element.1667) | copy-start | bytes 12292
  10.2 27.8 %copy-start.233 = (f32[4]{0:T(128)}, f32[4]{0:T(128)S(1)}, u32[]{:S(2)}) copy-start(f32[4]{0:T(128)S(1)} %get-tuple-element.1644) | copy-start | bytes 52
  10.2 30.3 %copy-start.235 = (f32[4]{0:T(128)}, f32[4]{0:T(128)S(1)}, u32[]{:S(2)}) copy-start(f32[4]{0:T(128)S(1)} %get-tuple-element.1645) | copy-start | bytes 52
  10.3 30.2 %copy-start.237 = (pred[128]{0:T(512)(128)(4,1)}, pred[128]{0:T(512)(128)(4,1)S(1)}, u32[]{:S(2)}) copy-start(pred[128]{0:T(512)(128)(4,1)S(1)} %get-tuple-element.1643) | copy-start | bytes 388
  10.3 121.5 %copy-start.198 = (pred[128]{0:T(512)(128)(4,1)}, pred[128]{0:T(512)(128)(4,1)S(1)}, u32[]{:S(2)}) copy-start(pred[128]{0:T(512)(128)(4,1)S(1)} %get-tuple-element.1642) | copy-start | bytes 388
  10.3 121.5 %copy-start.202 = (pred[128]{0:T(512)(128)(4,1)}, pred[128]{0:T(512)(128)(4,1)S(1)}, u32[]{:S(2)}) copy-start(pred[128]{0:T(512)(128)(4,1)S(1)} %get-tuple-element.1646) | copy-start | bytes 388
  10.3 121.5 %copy-start.206 = (pred[128]{0:T(512)(128)(4,1)}, pred[128]{0:T(512)(128)(4,1)S(1)}, u32[]{:S(2)}) copy-start(pred[128]{0:T(512)(128)(4,1)S(1)} %get-tuple-element.1647) | copy-start | bytes 388
  23.0 351.8 %copy-start.151 = (f32[1,1,1024]{2,1,0:T(1,128)}, f32[1,1,1024]{2,1,0:T(1,128)S(1)}, u32[]{:S(2)}) copy-start(f32[1,1,1024]{2,1,0:T(1,128)S(1)} %get-tuple-element.1629) | copy-start | bytes 12292
  23.0 468.9 %copy-start.149 = (f32[1,1,1024]{2,1,0:T(1,128)}, f32[1,1,1024]{2,1,0:T(1,128)S(1)}, u32[]{:S(2)}) copy-start(f32[1,1,1024]{2,1,0:T(1,128)S(1)} %get-tuple-element.1630) | copy-start | bytes 12292
  23.1 14.0 copy-start.271
  23.2 108.5 %copy-start.239 = (f32[128]{0:T(128)}, f32[128]{0:T(128)S(1)}, u32[]{:S(2)}) copy-start(f32[128]{0:T(128)S(1)} %fusion.515) | copy-start | bytes 1540
  36.9 455.1 %copy-start.159 = (bf16[1,1024,8]{1,2,0:T(8,128)(2,1)}, bf16[1,1024,8]{1,2,0:T(8,128)(2,1)S(1)}, u32[]{:S(2)}) copy-start(bf16[1,1024,8]{1,2,0:T(8,128)(2,1)S(1)} %all-gather.1) | copy-start | bytes 49156
  40.5 97.1 %copy-start.177 = (f32[4,2,64]{2,1,0:T(2,128)}, f32[4,2,64]{2,1,0:T(2,128)S(1)}, u32[]{:S(2)}) copy-start(f32[4,2,64]{2,1,0:T(2,128)S(1)} %get-tuple-element.1632) | copy-start | bytes 6148
  40.5 97.1 %copy-start.181 = (f32[4,2,64]{2,1,0:T(2,128)}, f32[4,2,64]{2,1,0:T(2,128)S(1)}, u32[]{:S(2)}) copy-start(f32[4,2,64]{2,1,0:T(2,128)S(1)} %get-tuple-element.1633) | copy-start | bytes 6148
  40.6 140.2 %copy-start.155 = (f32[4,2,64]{2,1,0:T(2,128)}, f32[4,2,64]{2,1,0:T(2,128)S(1)}, u32[]{:S(2)}) copy-start(f32[4,2,64]{2,1,0:T(2,128)S(1)} %mul.1564) | copy-start | bytes 6148
  40.6 91.2 %copy-start.164 = (f32[1,1,2048]{2,1,0:T(1,128)}, f32[1,1,2048]{2,1,0:T(1,128)S(1)}, u32[]{:S(2)}) copy-start(f32[1,1,2048]{2,1,0:T(1,128)S(1)} %get-tuple-element.1618) | copy-start | bytes 24580
  40.6 91.2 %copy-start.167 = (f32[1,1,2048]{2,1,0:T(1,128)}, f32[1,1,2048]{2,1,0:T(1,128)S(1)}, u32[]{:S(2)}) copy-start(f32[1,1,2048]{2,1,0:T(1,128)S(1)} %get-tuple-element.1619) | copy-start | bytes 24580
  40.6 91.2 %copy-start.170 = (f32[1,1,2048]{2,1,0:T(1,128)}, f32[1,1,2048]{2,1,0:T(1,128)S(1)}, u32[]{:S(2)}) copy-start(f32[1,1,2048]{2,1,0:T(1,128)S(1)} %get-tuple-element.1620) | copy-start | bytes 24580
  40.7 91.2 %copy-start.173 = (f32[1,1,2048]{2,1,0:T(1,128)}, f32[1,1,2048]{2,1,0:T(1,128)S(1)}, u32[]{:S(2)}) copy-start(f32[1,1,2048]{2,1,0:T(1,128)S(1)} %get-tuple-element.1621) | copy-start | bytes 24580
  137.4 44.5 %copy-start.59 = (f32[1,4,128,128]{3,1,2,0:T(4,128)}, f32[1,4,128,128]{3,1,2,0:T(4,128)S(1)}, u32[]{:S(2)}) copy-start(f32[1,4,128,128]{3,1,2,0:T(4,128)S(1)} %get-tuple-element.1663) | copy-start | bytes 786436
  139.9 41.1 %copy-start.80 = (f32[1,128,4,256]{3,2,1,0:T(4,128)}, f32[1,128,4,256]{3,2,1,0:T(4,128)S(1)}, u32[]{:S(2)}) copy-start(f32[1,128,4,256]{3,2,1,0:T(4,128)S(1)} %reshape.2328) | copy-start | bytes 1572868
  140.5 40.4 %copy-start.110 = (f32[4,2,64,64]{3,2,1,0:T(8,128)}, f32[4,2,64,64]{3,2,1,0:T(8,128)S(1)}, u32[]{:S(2)}) copy-start(f32[4,2,64,64]{3,2,1,0:T(8,128)S(1)} %fusion.360) | copy-start | bytes 393220
  185.2 10.1 copy-start.189
  192.3 9.4 copy-start.7
  192.3 9.4 copy-start.25
  192.3 9.4 copy-start.30
  192.3 9.4 copy-start.31
  192.3 9.4 copy-start.251
  192.3 9.4 copy-start.277
  201.8 179.1 %copy-start.275 = (f32[128]{0:T(128)}, f32[128]{0:T(128)S(1)}, u32[]{:S(2)}) copy-start(f32[128]{0:T(128)S(1)} %get-tuple-element.1648) | copy-start | bytes 1540
  201.8 279.4 %copy-start.2 = (f32[128,1024]{1,0:T(8,128)}, f32[128,1024]{1,0:T(8,128)S(1)}, u32[]{:S(2)}) copy-start(f32[128,1024]{1,0:T(8,128)S(1)} %get-tuple-element.1649) | copy-start | bytes 1572868
  201.8 179.0 %copy-start.241 = (f32[128]{0:T(128)}, f32[128]{0:T(128)S(1)}, u32[]{:S(2)}) copy-start(f32[128]{0:T(128)S(1)} %fusion.516) | copy-start | bytes 1540
  382.8 103.0 %copy-start.68 = (bf16[1,128,2816]{2,1,0:T(8,128)(2,1)}, bf16[1,128,2816]{2,1,0:T(8,128)(2,1)S(1)}, u32[]{:S(2)}) copy-start(bf16[1,128,2816]{2,1,0:T(8,128)(2,1)S(1)} %multiply_convert_fusion.1) | copy-start | bytes 2162692
  485.8 5.9 collective-permute-start
  506.8 64.0 %copy-start = (f32[1,4,128,128]{3,1,2,0:T(4,128)}, f32[1,4,128,128]{3,1,2,0:T(4,128)S(1)}, u32[]{:S(2)}) copy-start(f32[1,4,128,128]{3,1,2,0:T(4,128)S(1)} %bitcast_multiply_fusion.30) | copy-start | bytes 786436
  508.0 7.8 copy-start.66
  508.6 49.6 %copy-start.55 = (f32[1,4,128,128]{3,1,2,0:T(4,128)}, f32[1,4,128,128]{3,1,2,0:T(4,128)S(1)}, u32[]{:S(2)}) copy-start(f32[1,4,128,128]{3,1,2,0:T(4,128)S(1)} %fusion.391) | copy-start | bytes 786436
  514.0 44.2 %copy-start.114 = (f32[4,2,64,64]{3,2,1,0:T(8,128)}, f32[4,2,64,64]{3,2,1,0:T(8,128)S(1)}, u32[]{:S(2)}) copy-start(f32[4,2,64,64]{3,2,1,0:T(8,128)S(1)} %fusion.357) | copy-start | bytes 393220
  560.2 8.9 copy-start.54
  596.9 9.1 slice-start.10
  599.6 13.3 copy-start.12
  599.8 8.7 slice-start
  599.8 8.7 slice-start.1
  655.3 12.3 copy-start.109
  658.2 13.3 copy-start.100
  681.1 9.0 copy-start.166
  681.1 11.8 slice-start.6
  697.8 4.6 collective-permute-start.1
  699.3 8.3 slice-start.3
  768.0 8.6 copy-start.188
  768.1 12.1 slice-start.8
  770.1 7.5 copy-start.24
  796.1 7.4 copy-start.223
  796.2 7.6 copy-start.69
  857.5 576.0 %all-reduce.54.cloned.1.call-start = ((), (), s32[]{:S(2)}) async-start(), calls=%async_computation.2 | async-start | bytes 12976128 | tf_op jit(solution)/shard_map/psum | solution.py:340
  (280 other events, 923.1 us)
Sparse Core Ops, SparseCore 0:
  9.6 118.2 all-gather.10
  129.4 44.0 all-gather.12
  175.1 199.6 all-gather.14
  376.2 104.9 all-gather.16
  857.6 426.9 reduce-scatter.1
  1287.8 145.5 all-reduce.53
where the time goes:
time: 1470 us; the launch traced here: 1460 us
  waiting for transfers between devices  850 us (58%)
  other arithmetic  163 us (11%)
  local copies, waits for them, and re-layouts  161 us (11%)
  matrix products  151 us (10%)
  blocking collectives  106 us (7%)
  between operations  17.9 us (1%)
    reduce_scatter x1, waiting for transfers between devices, shards(): lax.psum_scatter(term_of(jnp.int32(0), own_rows * lax.axis_size('fsdp'))....  427 us
    all_gather x1, waiting for transfers between devices, shards(): lax.all_gather(up_weight[0], 'fsdp', axis=0, tiled=True)  173 us
    all_gather x1, waiting for transfers between devices, shards(): lax.all_gather(down_weight[0], 'fsdp', axis=0, tiled=True)  98.3 us
    all_gather x1, waiting for transfers between devices, shards(): lax.all_gather(proj_weight[0], 'fsdp', axis=0, tiled=True)  86.5 us
    another operation x6, other arithmetic, delta_rule(): lax.linalg.triangular_solve(system, right_side, left_side=True, lower=Tru...  83.3 us
    psum x1, blocking collectives, shards(): lax.psum((small_sum[0], small_sum[1], small_sum[2]), ('fsdp', 'dp'))  79.9 us
    psum x1, waiting for transfers between devices, shards(): totals = lax.psum(totals.astype(jnp.bfloat16), 'dp').astype(jnp.float32)  62.1 us
    concatenate x1, local copies, waits for them, and re-layouts, weight_terms(): jnp.concatenate([product(hidden_one, proj_cot), product(hidden_one, rate_...  48 us
  transfers between devices with their start and end apart: 8, of which 5 were waited for; matrix products, arithmetic and copies ran while one was open for 6% of the time, Pallas kernels for 0%

commit v1 on v0

--- a/solution.py
+++ b/solution.py
@@ -40,6 +40,44 @@
             * kernel[tap_count - 1 - offset]
         )
     return jax.nn.silu(total)
+
+
+@jax.custom_vjp
+def unit_solve(system, right_side):
+    return unit_solve_forward(system, right_side)[0]
+
+
+def unit_lower_inverse(system):
+    size = system.shape[-1]
+    places = jnp.arange(size)
+    inverse = None
+    half = 1
+    while half < size:
+        rows, columns = places[:, None] // half, places[None, :] // half
+        joins = (rows % 2 == 1) & (columns == rows - 1)
+        corner = jnp.where(joins, system, 0.0)
+        if inverse is None:
+            inverse = jnp.eye(size, dtype=system.dtype) - corner
+        else:
+            inner = jnp.matmul(corner, inverse, precision=highest)
+            inverse = inverse - jnp.matmul(inverse, inner, precision=highest)
+        half = half * 2
+    return inverse
+
+
+def unit_solve_forward(system, right_side):
+    inverse = unit_lower_inverse(system)
+    solved = jnp.matmul(inverse, right_side, precision=highest)
+    return solved, (inverse, solved)
+
+
+def unit_solve_backward(saved, cotangent):
+    inverse, solved = saved
+    right_cot = jnp.matmul(jnp.swapaxes(inverse, -1, -2), cotangent, precision=highest)
+    return -jnp.matmul(right_cot, jnp.swapaxes(solved, -1, -2), precision=highest), right_cot
+
+
+unit_solve.defvjp(unit_solve_forward, unit_solve_backward)
 
 
 def delta_rule(queries, key_rows, value_rows, beta_gate, decays, block_len):
@@ -65,9 +103,7 @@
     right_side = jnp.concatenate(
         [beta_keys * jnp.exp(levels)[..., None], value_rows * beta_gate[..., None]], -1
     )
-    solved = lax.linalg.triangular_solve(
-        system, right_side, left_side=True, lower=True, unit_diagonal=True
-    )
+    solved = unit_solve(system, right_side)
     solved_keys = solved[..., :key_dim]
     solved_values = solved[..., key_dim:]
     scores = jnp.einsum("bhncd,bhnmd->bhncm", queries, key_rows, precision=highest) * spread
@@ -93,7 +129,7 @@
         )
     )
     initial = jnp.zeros((batch_size, head_count, key_dim, value_dim), queries.dtype)
-    _, outputs = lax.scan(advance, initial, pieces)
+    _, outputs = lax.scan(advance, initial, pieces, unroll=block_count)
     return jnp.moveaxis(outputs, 0, 2).reshape(batch_size, head_count, length, value_dim)
 
 
@@ -139,13 +175,16 @@
 
 
 def layer_forward(entering, segment, weights, small_params):
-    norm_gains, proj_weight, rate_weight, out_weight, up_weight, down_weight = weights
+    norm_gains, first_weight, out_weight, up_weight, down_weight = weights
     kernel, head_params, out_gain = small_params
     widened = entering.astype(jnp.float32)
     normed_one, norm_one_back = jax.vjp(rms_gain, widened, norm_gains[0].astype(jnp.float32))
     hidden_one = normed_one.astype(jnp.bfloat16)
-    projected = jnp.dot(hidden_one, proj_weight, preferred_element_type=jnp.float32)
-    rate_logits = jnp.dot(hidden_one, rate_weight, preferred_element_type=jnp.float32)
+    joined = jnp.dot(hidden_one, first_weight, preferred_element_type=jnp.float32)
+    rates = 2 * head_params.shape[1]
+    proj_width = kernel.shape[1] + head_params.shape[1] * out_gain.shape[0]
+    projected = joined[..., :proj_width]
+    rate_logits = joined[..., proj_width : proj_width + rates]
     mixed_out, mixer_back = jax.vjp(
         partial(token_mixer, segment=segment), projected, rate_logits, kernel, head_params, out_gain
     )
@@ -171,7 +210,7 @@
 
 
 def layer_backward(cotangent_in, residuals, weights):
-    norm_gains, proj_weight, rate_weight, out_weight, up_weight, down_weight = weights
+    norm_gains, first_weight, out_weight, up_weight, down_weight = weights
     (
         norm_one_back,
         hidden_one,
@@ -193,12 +232,14 @@
     )
     proj_cot = proj_grad.astype(jnp.bfloat16)
     rate_cot = rate_grad.astype(jnp.bfloat16)
-    hidden_grad = last_contract(proj_cot, proj_weight) + last_contract(rate_cot, rate_weight)
+    used = proj_cot.shape[-1] + rate_cot.shape[-1]
+    spare = jnp.zeros(proj_cot.shape[:-1] + (first_weight.shape[1] - used,), jnp.bfloat16)
+    first_cot = jnp.concatenate([proj_cot, rate_cot, spare], -1)
+    hidden_grad = last_contract(first_cot, first_weight)
     entry_grad, gain_one = norm_one_back(hidden_grad)
     pairs = (
         hidden_one,
-        proj_cot,
-        rate_cot,
+        first_cot,
         mixed_half,
         branch_cot,
         hidden_two,
@@ -214,12 +255,11 @@
     )
 
 
-def weight_terms(pairs, gain_sum, start, count):
+def weight_terms(pairs, gain_sum):
     flattened = [member.reshape(-1, member.shape[-1]) for member in pairs]
     (
         hidden_one,
-        proj_cot,
-        rate_cot,
+        first_cot,
         mixed_half,
         branch_cot,
         hidden_two,
@@ -233,25 +273,40 @@
             left, right, (((0,), (0,)), ((), ())), preferred_element_type=jnp.float32
         )
 
-    return jnp.concatenate(
-        [
-            product(hidden_one, proj_cot),
-            product(hidden_one, rate_cot),
-            product(branch_cot, mixed_half),
-            product(hidden_two, gate_up_cot),
-            product(dout_half, act_half),
-            gain_sum.T,
-        ],
-        1,
-    )
-
-
-def split_term(total, widths):
+    first = product(hidden_one, first_cot)
+    first = jnp.concatenate([first[:, : -gain_sum.shape[0]], gain_sum.T], 1)
+    return (
+        product(dout_half, act_half),
+        product(hidden_two, gate_up_cot),
+        product(branch_cot, mixed_half),
+        first,
+    )
+
+
+group = ("fsdp", "dp")
+
+
+def gathered(shard):
+    count = shard.shape[0] // lax.axis_size("dp")
+    part = lax.dynamic_slice_in_dim(shard, lax.axis_index("dp") * count, count, 0)
+    return lax.all_gather(part, group, axis=0, tiled=True)
+
+
+def scattered(term):
+    part = lax.psum_scatter(term.astype(jnp.bfloat16), group, scatter_dimension=0, tiled=True)
+    return lax.all_gather(part, "dp", axis=0, tiled=True).astype(jnp.float32)
+
+
+def summed_small(arrays):
+    flat = jnp.concatenate([array.reshape(-1) for array in arrays])
+    padded = jnp.pad(flat, (0, -flat.size % 1024)).reshape(-1, 128)
+    members = lax.all_gather(padded, group, axis=0, tiled=True)
+    total = jnp.sum(members.reshape((-1,) + padded.shape), 0).reshape(-1)
     pieces = []
-    column = 0
-    for width in widths:
-        pieces.append(total[..., column : column + width])
-        column = column + width
+    place = 0
+    for array in arrays:
+        pieces.append(total[place : place + array.size].reshape(array.shape))
+        place = place + array.size
     return pieces
 
 
@@ -278,13 +333,15 @@
     out_gain,
 ):
     first_section = lax.axis_index("section") == 0
+    first_weight = gathered(
+        jnp.concatenate([proj_weight[0], rate_weight[0], norm_gains[0].T], 1)
+    )
     weights = (
-        lax.all_gather(norm_gains[0], "fsdp", axis=1, tiled=True),
-        lax.all_gather(proj_weight[0], "fsdp", axis=0, tiled=True),
-        lax.all_gather(rate_weight[0], "fsdp", axis=0, tiled=True),
-        lax.all_gather(out_weight[0], "fsdp", axis=0, tiled=True),
-        lax.all_gather(up_weight[0], "fsdp", axis=0, tiled=True),
-        lax.all_gather(down_weight[0], "fsdp", axis=0, tiled=True),
+        first_weight[:, -norm_gains.shape[1] :].T,
+        first_weight,
+        gathered(out_weight[0]),
+        gathered(up_weight[0]),
+        gathered(down_weight[0]),
     )
     small_params = (conv_kernels[0], head_params[0], out_gain[0])
     batches = tokens.shape[0]
@@ -322,43 +379,29 @@
         kept_pairs.append(pairs)
         small_list.append(small_grads)
         gain_list.append(gains_step)
-    pairs_all = tuple((jnp.concatenate([member[i] for member in kept_pairs], 1) for i in range(9)))
+    if batches == 1:
+        pairs_all = tuple((jnp.where(first_section, b, a) for a, b in zip(*kept_pairs)))
+    else:
+        pairs_all = tuple((jnp.concatenate(members, 1) for members in zip(*kept_pairs)))
     gain_sum = sum(gain_list)
     small_sum = tuple((sum((member[i] for member in small_list)) for i in range(3)))
     section_output = jnp.stack([jnp.where(first_section, results[0], results[1])])[None]
     input_grad = jnp.stack([jnp.where(first_section, incoming[batches], incoming[batches - 1])])[
         None
     ]
-    own_rows = proj_weight.shape[1]
-    term_of = partial(weight_terms, pairs_all, gain_sum)
-    totals = lax.psum_scatter(
-        term_of(jnp.int32(0), own_rows * lax.axis_size("fsdp")).astype(jnp.bfloat16),
-        "fsdp",
-        scatter_dimension=0,
-        tiled=True,
-    ).astype(jnp.float32)
-    totals = lax.psum(totals.astype(jnp.bfloat16), "dp").astype(jnp.float32)
-    kernel_grad, head_grad, out_gain_grad = lax.psum(
-        (small_sum[0], small_sum[1], small_sum[2]), ("fsdp", "dp")
-    )
-    widths = [
-        proj_weight.shape[2],
-        rate_weight.shape[2],
-        out_weight.shape[2],
-        up_weight.shape[2],
-        down_weight.shape[2],
-        2,
-    ]
-    pieces = split_term(totals, widths)
+    down_grad, up_grad, out_grad, first_grad = map(scattered, weight_terms(pairs_all, gain_sum))
+    kernel_grad, head_grad, out_gain_grad = summed_small(small_sum)
+    proj_width = proj_weight.shape[2]
+    used = proj_width + rate_weight.shape[2]
     return (
         section_output,
         input_grad,
-        pieces[5].T[None],
-        pieces[0][None],
-        pieces[1][None],
-        pieces[2][None],
-        pieces[3][None],
-        pieces[4][None],
+        first_grad[:, used:].T[None],
+        first_grad[:, :proj_width][None],
+        first_grad[:, proj_width:used][None],
+        out_grad[None],
+        up_grad[None],
+        down_grad[None],
         kernel_grad[None],
         head_grad[None],
         out_gain_grad[None],

time: 1470 us -> 1290 us (0.88)
  local copies, waits for them, and re-layouts: 161 us -> 79.9 us
  other arithmetic: 163 us -> 87 us
  blocking collectives: 106 us -> 57.6 us
  waiting for transfers between devices: 850 us -> 876 us
    psum x1 -> x0, blocking collectives: 79.9 us -> none  [shards(): lax.psum((small_sum[0], small_sum[1], small_sum[2]), ('fsdp', 'dp'))]
    another operation x6 -> x3, other arithmetic: 83.3 us -> 5.68 us  [delta_rule(): lax.linalg.triangular_solve(system, right_side, left_side=True, lower=Tru...]
    all_gather x4 -> x7, waiting for transfers between devices: 358 us -> 422 us  [the longest x4 338 us: gathered(): return lax.all_gather(part, group, axis=0, tiled=True)]
    psum x1 -> x0, waiting for transfers between devices: 62.1 us -> none  [shards(): totals = lax.psum(totals.astype(jnp.bfloat16), 'dp').astype(jnp.float32)]
    concatenate x1 -> x3, local copies, waits for them, and re-layouts: 48 us -> 4.44 us  [the longest x1 3.69 us: shards(): jnp.concatenate([proj_weight[0], rate_weight[0], norm_gains[0].T], 1)]
    all_gather x2, blocking collectives: 26.4 us -> 57.6 us  [the longest x1 48.2 us: summed_small(): members = lax.all_gather(padded, group, axis=0, tiled=True)]
    reduce_scatter x1 -> x4, waiting for transfers between devices: 427 us -> 453 us  [scattered(): lax.psum_scatter(term.astype(jnp.bfloat16), group, scatter_dimension=0, t...]
    another operation x24 -> x2, local copies, waits for them, and re-layouts: 16.2 us -> 0.63 us  [the longest x1 0.63 us: shards(): kernel_grad[None]]
  transfers between devices with their start and end apart: 8 -> 13, of which waited for: 5 -> 12; matrix products, arithmetic and copies ran while one was open for 6% -> 13% of each run, Pallas kernels for 0% -> 0%
where the time goes in v1:
time: 1290 us; the launch traced here: 1280 us
  waiting for transfers between devices  876 us (68%)
  matrix products  159 us (12%)
  other arithmetic  87 us (7%)
  local copies, waits for them, and re-layouts  79.9 us (6%)
  blocking collectives  57.6 us (4%)
  between operations  17.7 us (1%)
    reduce_scatter x4, waiting for transfers between devices, scattered(): lax.psum_scatter(term.astype(jnp.bfloat16), group, scatter_dimension=0, t...  453 us
    all_gather x4, waiting for transfers between devices, gathered(): return lax.all_gather(part, group, axis=0, tiled=True)  338 us
    all_gather x3, waiting for transfers between devices, scattered(): return lax.all_gather(part, 'dp', axis=0, tiled=True).astype(jnp.float32)  84.2 us
    all_gather x1, blocking collectives, summed_small(): members = lax.all_gather(padded, group, axis=0, tiled=True)  48.2 us
    dot_general x8, matrix products, last_contract(): lax.dot_general(left, right, (((2,), (1,)), ((), ())), preferred_element_...  40.4 us
    unnamed x413, local copies, waits for them, and re-layouts  26.6 us
  transfers between devices with their start and end apart: 13, of which 12 were waited for; matrix products, arithmetic and copies ran while one was open for 13% of the time, Pallas kernels for 0%

profile of v1, /device:TPU:0, one launch (start us, length us, event | category | flops | bytes accessed | tf_op | source)
XLA Modules:
  0.0 1281.1 jit_solution(4349400596759229962)
XLA Ops:
  10.7 3.7 concatenate.84
  14.4 1.8 constant_dynamic-slice_fusion.3
  21.9 52.7 %all-gather.19.cloned.1.call-done = bf16[1,1024,1024]{2,1,0:T(8,128)(2,1)} async-done(((bf16[1,64,1024]{2,1,0:T(8,128)(2,1)}), bf16[1,1024,1024]{2,1,0:T(8,128)(2,1)}) %all-gather.19.cloned.1.call-update) | async-done | bytes 2097168 | tf_op jit(solution)/shard_map/all_gather | solution.py:292
  74.6 3.9 copy.456
  78.5 94.1 %all-gather.11.cloned.1.call-done = bf16[1024,3082]{1,0:T(8,128)(2,1)} async-done(((bf16[64,3082]{1,0:T(8,128)(2,1)}), bf16[1024,3082]{1,0:T(8,128)(2,1)}) %all-gather.11.cloned.1.call-update) | async-done | bytes 6311952 | tf_op jit(solution)/shard_map/all_gather | solution.py:292
  174.6 5.5 convolution_bitcast_fusion.1
  180.2 4.2 fusion.113
  203.3 2.6 multiply_reduce_fusion.18
  206.0 109.9 %all-gather.21.cloned.1.call-done = bf16[1,1024,5632]{2,1,0:T(8,128)(2,1)} async-done(((bf16[1,64,5632]{2,1,0:T(8,128)(2,1)}), bf16[1,1024,5632]{2,1,0:T(8,128)(2,1)}) %all-gather.21.cloned.1.call-update) | async-done | bytes 11534352 | tf_op jit(solution)/shard_map/all_gather | solution.py:292
  315.9 6.4 fusion.8
  324.3 81.6 %all-gather.23.cloned.1.call-done = bf16[1,1024,2816]{2,1,0:T(8,128)(2,1)} async-done(((bf16[1,64,2816]{2,1,0:T(8,128)(2,1)}), bf16[1,1024,2816]{2,1,0:T(8,128)(2,1)}) %all-gather.23.cloned.1.call-update) | async-done | bytes 5767184 | tf_op jit(solution)/shard_map/all_gather | solution.py:292
  406.0 4.6 fusion.71
  414.8 5.7 convolution_bitcast_fusion
  421.5 4.0 fusion.112
  446.8 2.1 select_bitcast_fusion
  449.2 2.6 multiply_reduce_fusion.16
  451.9 6.3 fusion.11
  458.3 3.2 fusion.316
  461.4 7.0 fusion.174
  491.1 2.2 slice_multiply_fusion.1
  493.3 2.2 multiply_reduce_fusion.27
  495.7 2.0 multiply_bitcast_fusion.1
  498.2 1.8 reduce_window_sum.42
  503.0 2.2 fusion.84
  508.0 1.9 copy.474
  514.8 3.0 multiply_select_fusion.3
  517.8 2.4 multiply_select_fusion.4
  520.2 2.1 copy.457
  522.3 3.1 fusion.108
  526.3 6.7 fusion.151
  534.1 2.0 collective-permute-start.1
  537.8 3.0 fusion.315
  540.8 7.0 multiply_reduce_fusion.10
  549.2 2.6 convolution_bitcast_fusion.4
  553.7 4.2 convolution_convert_fusion.1
  562.1 1.9 fusion.178
  564.6 1.8 fusion.176
  572.7 2.5 multiply_reduce_fusion.23
  579.4 1.9 multiply_bitcast_fusion
  583.3 2.0 reduce_window_sum.43
  597.8 7.6 multiply_reduce_fusion.3
  607.2 1.8 fusion.111
  610.3 3.8 fusion.122
  614.2 2.9 copy-done.2
  617.7 4.4 fusion.153
  622.1 3.3 pad_maximum_fusion
  625.4 8.9 copy.571
  635.1 9.1 convolution_convert_fusion
  645.4 2.1 convolution_convert_fusion.2
  647.5 35.7 %reduce-scatter.11.cloned.1.call-done = bf16[64,2816]{1,0:T(8,128)(2,1)} async-done(((bf16[1024,2816]{1,0:T(8,128)(2,1)}), bf16[64,2816]{1,0:T(8,128)(2,1)}) %reduce-scatter.11.cloned.1.call-update) | async-done | bytes 360464 | tf_op jit(solution)/shard_map/reduce_scatter | solution.py:296
  683.3 144.6 %reduce-scatter.13.cloned.1.call-done = bf16[64,3082]{1,0:T(8,128)(2,1)} async-done(((bf16[1024,3082]{1,0:T(8,128)(2,1)}), bf16[64,3082]{1,0:T(8,128)(2,1)}) %reduce-scatter.13.cloned.1.call-update) | async-done | bytes 394512 | tf_op jit(solution)/shard_map/reduce_scatter | solution.py:296
  827.9 244.6 %reduce-scatter.9.cloned.1.call-done = bf16[64,5632]{1,0:T(8,128)(2,1)} async-done(((bf16[1024,5632]{1,0:T(8,128)(2,1)}), bf16[64,5632]{1,0:T(8,128)(2,1)}) %reduce-scatter.9.cloned.1.call-update) | async-done | bytes 720912 | tf_op jit(solution)/shard_map/reduce_scatter | solution.py:296
  1072.6 5.5 fusion.93
  1078.4 48.2 %all_gather.35 = f32[1152,128]{1,0:T(8,128)S(1)} all-gather(f32[72,128]{1,0:T(8,128)S(1)} %pad_bitcast_fusion), channel_id=1, replica_groups=mesh['section'=2,'fsdp'=4,'dp'=4] {'fsdp','dp'}, dimensions={0}, use_global_device_ids=true | all-gather | bytes 626688 | tf_op jit(solution)/shard_map/all_gather | solution.py:303
  1126.6 2.8 slice.358
  1132.0 1.8 fusion.170
  1133.8 27.9 %reduce-scatter.7.cloned.1.call-done = bf16[64,1024]{1,0:T(8,128)(2,1)} async-done(((bf16[1024,1024]{1,0:T(8,128)(2,1)}), bf16[64,1024]{1,0:T(8,128)(2,1)}) %reduce-scatter.7.cloned.1.call-update) | async-done | bytes 131088 | tf_op jit(solution)/shard_map/reduce_scatter | solution.py:296
  1161.7 9.4 all_gather.32
  1172.2 20.3 %all-gather.17.cloned.1.call-done = bf16[256,2816]{1,0:T(8,128)(2,1)} async-done(((bf16[64,2816]{1,0:T(8,128)(2,1)}), bf16[256,2816]{1,0:T(8,128)(2,1)}) %all-gather.17.cloned.1.call-update) | async-done | bytes 1441808 | tf_op jit(solution)/shard_map/all_gather | solution.py:297
  1192.4 3.1 bitcast_convert_fusion.1
  1195.6 30.0 %all-gather.13.cloned.1.call-done = bf16[256,3082]{1,0:T(8,128)(2,1)} async-done(((bf16[64,3082]{1,0:T(8,128)(2,1)}), bf16[256,3082]{1,0:T(8,128)(2,1)}) %all-gather.13.cloned.1.call-update) | async-done | bytes 1578000 | tf_op jit(solution)/shard_map/all_gather | solution.py:297
  1231.2 3.9 slice_bitcast_fusion
  1235.1 34.0 %all-gather.15.cloned.1.call-done = bf16[256,5632]{1,0:T(8,128)(2,1)} async-done(((bf16[64,5632]{1,0:T(8,128)(2,1)}), bf16[256,5632]{1,0:T(8,128)(2,1)}) %all-gather.15.cloned.1.call-update) | async-done | bytes 2883600 | tf_op jit(solution)/shard_map/all_gather | solution.py:297
  1269.1 5.2 bitcast_convert_fusion
  (740 shorter events, 142.4 us)
Async XLA Ops:
  7.2 9.1 copy-start
  7.2 67.4 %all-gather.19.cloned.1.call-start = ((), (), s32[]{:S(2)}) async-start(), calls=%async_computation.11 | async-start | bytes 2228224 | tf_op jit(solution)/shard_map/all_gather | solution.py:292
  9.0 163.6 %all-gather.11.cloned.1.call-start = ((), (), s32[]{:S(2)}) async-start(), calls=%async_computation.4 | async-start | bytes 6963200 | tf_op jit(solution)/shard_map/all_gather | solution.py:292
  16.2 299.7 %all-gather.21.cloned.1.call-start = ((), (), s32[]{:S(2)}) async-start(), calls=%async_computation.12 | async-start | bytes 12255232 | tf_op jit(solution)/shard_map/all_gather | solution.py:292
  17.2 388.8 %all-gather.23.cloned.1.call-start = ((), (), s32[]{:S(2)}) async-start(), calls=%async_computation.13 | async-start | bytes 6127616 | tf_op jit(solution)/shard_map/all_gather | solution.py:292
  19.0 664.2 %reduce-scatter.11.cloned.1.call-start = ((), (), s32[]{:S(2)}) async-start(), calls=%async_computation.9 | async-start | bytes 6127616 | tf_op jit(solution)/shard_map/reduce_scatter | solution.py:296
  19.4 59.2 %copy-start.186 = (f32[128]{0:T(128)}, f32[128]{0:T(128)S(1)}, u32[]{:S(2)}) copy-start(f32[128]{0:T(128)S(1)} %fusion.154) | copy-start | bytes 1540
  19.4 155.2 %copy-start.174 = (f32[128]{0:T(128)}, f32[128]{0:T(128)S(1)}, u32[]{:S(2)}) copy-start(f32[128]{0:T(128)S(1)} %fusion.409) | copy-start | bytes 1540
  20.0 400.5 %copy-start.156 = (pred[128]{0:T(512)(128)(4,1)}, pred[128]{0:T(512)(128)(4,1)S(1)}, u32[]{:S(2)}) copy-start(pred[128]{0:T(512)(128)(4,1)S(1)} %get-tuple-element.187) | copy-start | bytes 388
  20.7 399.9 %copy-start.159 = (f32[4]{0:T(128)}, f32[4]{0:T(128)S(1)}, u32[]{:S(2)}) copy-start(f32[4]{0:T(128)S(1)} %get-tuple-element.185) | copy-start | bytes 52
  20.7 399.9 %copy-start.162 = (f32[4]{0:T(128)}, f32[4]{0:T(128)S(1)}, u32[]{:S(2)}) copy-start(f32[4]{0:T(128)S(1)} %get-tuple-element.186) | copy-start | bytes 52
  21.6 169.7 %copy-start.169 = (pred[64,64]{1,0:T(8,128)(4,1)}, pred[64,64]{1,0:T(8,128)(4,1)S(1)}, u32[]{:S(2)}) copy-start(pred[64,64]{1,0:T(8,128)(4,1)S(1)} %compare_and_fusion.4) | copy-start | bytes 12292
  180.1 6.9 copy-start.12
  187.9 8.2 copy-start.52
  189.4 8.5 copy-start.38
  190.4 8.9 copy-start.96
  190.4 9.6 copy-start.92
  200.9 211.0 %copy-start.60 = (f32[4,64,256]{2,1,0:T(8,128)}, f32[4,64,256]{2,1,0:T(8,128)S(1)}, u32[]{:S(2)}) copy-start(f32[4,64,256]{2,1,0:T(8,128)S(1)} %convolution_subtract_fusion.12) | copy-start | bytes 786436
  205.9 116.4 %copy-start.190 = (f32[128]{0:T(128)}, f32[128]{0:T(128)S(1)}, u32[]{:S(2)}) copy-start(f32[128]{0:T(128)S(1)} %get-tuple-element.191) | copy-start | bytes 1540
  206.0 116.4 %copy-start.148 = (f32[128]{0:T(128)}, f32[128]{0:T(128)S(1)}, u32[]{:S(2)}) copy-start(f32[128]{0:T(128)S(1)} %fusion.410) | copy-start | bytes 1540
  324.3 86.2 %copy-start.50 = (bf16[1,128,2816]{2,1,0:T(8,128)(2,1)}, bf16[1,128,2816]{2,1,0:T(8,128)(2,1)S(1)}, u32[]{:S(2)}) copy-start(bf16[1,128,2816]{2,1,0:T(8,128)(2,1)S(1)} %multiply_convert_fusion.1) | copy-start | bytes 2162692
  324.3 89.3 %copy-start.97 = (f32[2,1,4,64,128]{4,3,2,1,0:T(8,128)S(1)}, f32[2,1,4,64,128]{4,3,2,1,0:T(8,128)}, u32[]{:S(2)}) copy-start(f32[2,1,4,64,128]{4,3,2,1,0:T(8,128)} %copy-done.96) | copy-start | bytes 786436
  410.6 9.9 copy-start.113
  410.6 4.0 collective-permute-start
  414.7 5.7 copy-start.188
  414.7 34.4 %copy-start.19 = (bf16[1,128,1024]{2,1,0:T(8,128)(2,1)}, bf16[1,128,1024]{2,1,0:T(8,128)(2,1)S(1)}, u32[]{:S(2)}) copy-start(bf16[1,128,1024]{2,1,0:T(8,128)(2,1)S(1)} %get-tuple-element.128) | copy-start | bytes 786436
  427.5 14.6 %copy-start.46 = (f32[1,4,128,128]{3,2,1,0:T(8,128)}, f32[1,4,128,128]{3,2,1,0:T(8,128)S(1)}, u32[]{:S(2)}) copy-start(f32[1,4,128,128]{3,2,1,0:T(8,128)S(1)} %fusion.235) | copy-start | bytes 786436
  432.2 6.2 copy-start.54
  449.1 9.1 slice-start.9
  451.8 16.6 %copy-start.130 = (f32[128]{0:T(128)}, f32[128]{0:T(128)S(1)}, u32[]{:S(2)}) copy-start(f32[128]{0:T(128)S(1)} %fusion.412) | copy-start | bytes 1540
  451.8 6.4 slice-start.10
  451.8 6.4 copy-start.63
  451.8 9.6 slice-start
  451.9 9.6 slice-start.1
  469.8 63.2 %copy-start.5 = (f32[1,128,1024]{2,1,0:T(8,128)}, f32[1,128,1024]{2,1,0:T(8,128)S(1)}, u32[]{:S(2)}) copy-start(f32[1,128,1024]{2,1,0:T(8,128)S(1)} %fusion.157) | copy-start | bytes 1572868
  497.7 7.4 copy-start.80
  498.1 8.9 copy-start.45
  525.4 12.4 slice-start.11
  526.3 6.7 copy-start.189
  526.3 11.5 slice-start.12
  526.3 14.5 %slice-start.3 = ((s8[11534336]{0:T(1024)(128)(4,1)}), s8[4194304]{0:T(1024)(128)(4,1)S(1)}, s32[]{:S(2)}) async-start(s8[11534336]{0:T(1024)(128)(4,1)} %bitcast.1185), calls=%async_computation.18 | async-start | bytes 8388608
  533.0 7.8 slice-start.4
  534.1 3.7 collective-permute-start.1
  540.8 7.0 copy-start.191
  558.0 269.9 %reduce-scatter.13.cloned.1.call-start = ((), (), s32[]{:S(2)}) async-start(), calls=%async_computation.14 | async-start | bytes 6963200 | tf_op jit(solution)/shard_map/reduce_scatter | solution.py:296
  559.8 6.6 copy-start.13
  572.7 6.6 copy-start.8
  581.3 6.3 copy-start.79
  581.3 6.3 copy-start.105
  581.3 6.4 copy-start.124
  582.5 6.9 copy-start.37
  610.3 6.9 slice-start.6
  634.4 438.1 %reduce-scatter.9.cloned.1.call-start = ((), (), s32[]{:S(2)}) async-start(), calls=%async_computation.7 | async-start | bytes 12255232 | tf_op jit(solution)/shard_map/reduce_scatter | solution.py:296
  644.1 517.5 %reduce-scatter.7.cloned.1.call-start = ((), (), s32[]{:S(2)}) async-start(), calls=%async_computation.6 | async-start | bytes 2228224 | tf_op jit(solution)/shard_map/reduce_scatter | solution.py:296
  647.5 425.0 %copy-start.114 = (bf16[1,128,1024]{2,1,0:T(8,128)(2,1)S(1)}, bf16[1,128,1024]{2,1,0:T(8,128)(2,1)}, u32[]{:S(2)}) copy-start(bf16[1,128,1024]{2,1,0:T(8,128)(2,1)} %copy-done.113) | copy-start | bytes 786436
  647.5 544.9 %all-gather.17.cloned.1.call-start = ((), (), s32[]{:S(2)}) async-start(), calls=%async_computation.10 | async-start | bytes 1802240 | tf_op jit(solution)/shard_map/all_gather | solution.py:297
  683.3 542.3 %all-gather.13.cloned.1.call-start = ((), (), s32[]{:S(2)}) async-start(), calls=%async_computation.5 | async-start | bytes 2048000 | tf_op jit(solution)/shard_map/all_gather | solution.py:297
  827.9 441.2 %all-gather.15.cloned.1.call-start = ((), (), s32[]{:S(2)}) async-start(), calls=%async_computation.8 | async-start | bytes 3604480 | tf_op jit(solution)/shard_map/all_gather | solution.py:297
  1072.5 5.8 copy-start.176
  1072.5 5.8 copy-start.177
  1078.1 53.9 %copy-start.187 = (f32[128]{0:T(128)S(1)}, f32[128]{0:T(128)}, u32[]{:S(2)}) copy-start(f32[128]{0:T(128)} %copy-done.186) | copy-start | bytes 1540
  1078.1 53.9 %copy-start.89 = (f32[128,1024]{1,0:T(8,128)S(1)}, f32[128,1024]{1,0:T(8,128)}, u32[]{:S(2)}) copy-start(f32[128,1024]{1,0:T(8,128)} %copy-done.88) | copy-start | bytes 1572868
  1078.1 53.9 %copy-start.119 = (f32[128,1024]{1,0:T(8,128)S(1)}, f32[128,1024]{1,0:T(8,128)}, u32[]{:S(2)}) copy-start(f32[128,1024]{1,0:T(8,128)} %get-tuple-element.212) | copy-start | bytes 1572868
  1078.1 53.9 %copy-start.183 = (f32[128]{0:T(128)S(1)}, f32[128]{0:T(128)}, u32[]{:S(2)}) copy-start(f32[128]{0:T(128)} %copy-done.182) | copy-start | bytes 1540
  (156 other events, 432.3 us)
Sparse Core Ops, SparseCore 0:
  11.3 63.2 all-gather.18
  77.9 94.6 all-gather.10
  175.9 139.9 all-gather.20
  319.0 86.9 all-gather.22
  558.1 125.0 reduce-scatter.10
  685.4 142.4 reduce-scatter.12
  830.1 242.2 reduce-scatter.8
  1075.3 86.3 reduce-scatter.6
  1163.5 28.8 all-gather.16
  1194.1 31.3 all-gather.12
  1227.4 41.6 all-gather.14
